TPU v7x, 512 devices: a whole 4x8x8 slice. The times are simulated.
512 devices in a mesh: group: 64 (over y_lo, z, core), tensor: 8 (over y_hi, x).
Axes of the slice: x: 4, y: 8 (y_hi: 2, y_lo: 4; y = y_hi * 4 + y_lo), z: 8, core: 2. Of those that a mesh axis runs over, the one named last changes fastest.
Arguments:
- turns: bfloat16 [64, 1024, 4096], P('group', 'tensor'), may hold values from -16 to 16
- query_store: bfloat16 [64, 64, 4096], P('group', None, 'tensor'), may hold values from -0.09375 to 0.09375
- key_block_holder: bfloat16 [64, 64, 4, 128], P('group'), may hold values from -0.09375 to 0.09375
- value_block_holder: bfloat16 [64, 64, 4, 128], P('group'), may hold values from -0.09375 to 0.09375
- query_bias: float32 [4096], P('tensor'), may hold values from -3 to 3
- key_projection_bias: float32 [512], replicated, may hold values from -3 to 3
- value_projection_bias: float32 [512], replicated, may hold values from -3 to 3
- owner: int32 [64], replicated, may hold values from 0 to 63, each once
- lengths: int32 [64], P('group'), may hold values from 1 to 1024, as said below
Outputs:
- attended: bfloat16 [64, 1024, 4096], P('group', None, 'tensor')
Inputs may be any that keep to these rules, and one draw needn't show every extreme that they name: `owner`: each group index holds exactly one block. `lengths`: some group's turn fills all 1024 positions.
All inputs are finite; a program needn't handle non-finite values.
Results may differ from a plain program's by a relative error of at most 0.0055.
The roundings to bfloat16 on the way count: a program that leaves them out, or rounds other values in their place, can miss the bound.
Values may be sent and summed in bfloat16 or wider, within the bound.
No kernel may reach another device: no remote copies, remote signals or barrier semaphores. Data moves between devices by JAX's collectives and lax.ppermute only.
A program may use at most 128 MiB of HBM per device.

v0:
```python
import jax
import jax.numpy as jnp
from jax import lax
from jax.sharding import PartitionSpec as P

QUERY_HEADS = 32
KEY_VALUE_HEADS = 4
HEAD_SIZE = 128
rotary_base = 1000000.0


def rotary(heads, positions):
    half = heads.shape[-1] // 2
    expo = jnp.arange(half, dtype=jnp.float32) * 2.0 / heads.shape[-1]
    freqs = rotary_base ** (-expo)
    angles = positions[:, None] * freqs[None, :]
    cosine = jnp.cos(angles)[None]
    sine = jnp.sin(angles)[None]
    first = heads[..., :half]
    second = heads[..., half:]
    return jnp.concatenate(
        [first * cosine - second * sine, second * cosine + first * sine], axis=-1
    )


def per_device(
    turns,
    query_store,
    key_block_holder,
    value_block_holder,
    query_bias,
    key_projection_bias,
    value_projection_bias,
    owner,
    lengths,
):
    tensor_index = lax.axis_index("tensor")
    group_count = lax.axis_size("group")
    gathered = lax.all_gather(turns, "tensor", axis=1, tiled=True)[0]
    token_count = gathered.shape[0]
    block_rows = query_store.shape[1]
    query_cols = query_store.shape[2]
    heads_dev = query_cols // HEAD_SIZE
    query_per_key_head = QUERY_HEADS // KEY_VALUE_HEADS
    key_value_per_group = max(1, heads_dev // query_per_key_head)
    key_value_leading = tensor_index * heads_dev // query_per_key_head
    keys_mine = lax.dynamic_slice_in_dim(
        key_block_holder, key_value_leading, key_value_per_group, 2
    ).reshape(1, block_rows, key_value_per_group * HEAD_SIZE)
    values_mine = lax.dynamic_slice_in_dim(
        value_block_holder, key_value_leading, key_value_per_group, 2
    ).reshape(1, block_rows, key_value_per_group * HEAD_SIZE)
    inverse = (
        jnp.zeros((group_count,), jnp.int32).at[owner].set(jnp.arange(group_count, dtype=jnp.int32))
    )
    ordered = jnp.take(gathered.reshape(token_count, group_count, block_rows), inverse, axis=1)
    proj_query = jnp.einsum(
        "tgc,gcn->tn",
        ordered,
        lax.all_gather(query_store, "group", axis=0, tiled=True),
        preferred_element_type=jnp.float32,
    )
    proj_key = jnp.einsum(
        "tgc,gcn->tn",
        ordered,
        lax.all_gather(keys_mine, "group", axis=0, tiled=True),
        preferred_element_type=jnp.float32,
    )
    proj_value = jnp.einsum(
        "tgc,gcn->tn",
        ordered,
        lax.all_gather(values_mine, "group", axis=0, tiled=True),
        preferred_element_type=jnp.float32,
    )
    key_bias_rows = lax.dynamic_slice_in_dim(
        key_projection_bias.reshape(KEY_VALUE_HEADS, HEAD_SIZE),
        key_value_leading,
        key_value_per_group,
        0,
    ).reshape(key_value_per_group * HEAD_SIZE)
    bias_values = lax.dynamic_slice_in_dim(
        value_projection_bias.reshape(KEY_VALUE_HEADS, HEAD_SIZE),
        key_value_leading,
        key_value_per_group,
        0,
    ).reshape(key_value_per_group * HEAD_SIZE)
    positions = jnp.arange(token_count, dtype=jnp.float32)
    raw_query = (
        (proj_query + query_bias).reshape(token_count, heads_dev, HEAD_SIZE).transpose(1, 0, 2)
    )
    unbiased_key = (
        (proj_key + key_bias_rows)
        .reshape(token_count, key_value_per_group, HEAD_SIZE)
        .transpose(1, 0, 2)
    )
    unbiased_value = (
        (proj_value + bias_values)
        .reshape(token_count, key_value_per_group, HEAD_SIZE)
        .transpose(1, 0, 2)
    )
    queries = rotary(raw_query, positions).astype(jnp.bfloat16)
    keys_rot = rotary(unbiased_key, positions).astype(jnp.bfloat16)
    values_cast = unbiased_value.astype(jnp.bfloat16)
    repeat_count = heads_dev // key_value_per_group
    keys_full = jnp.repeat(keys_rot, repeat_count, axis=0)
    values_full = jnp.repeat(values_cast, repeat_count, axis=0)
    index = jnp.arange(token_count, dtype=jnp.int32)
    span = min(256, token_count)
    outputs = []
    for block in range(token_count // span):
        first = block * span
        last = first + span
        scores = jnp.einsum(
            "htd,hsd->hts",
            queries[:, first:last],
            keys_full[:, :last],
            preferred_element_type=jnp.float32,
        ) * HEAD_SIZE ** (-0.5)
        causal = index[None, :last] <= index[first:last, None]
        scores = jnp.where(causal[None], scores, -jnp.inf)
        top = jnp.max(scores, axis=-1, keepdims=True)
        expd = jnp.exp(scores - top)
        weights = (expd / jnp.sum(expd, axis=-1, keepdims=True)).astype(jnp.bfloat16)
        outputs.append(
            jnp.einsum(
                "hts,hsd->htd", weights, values_full[:, :last], preferred_element_type=jnp.float32
            )
        )
    mixed = jnp.concatenate(outputs, axis=1)
    mixed = mixed.transpose(1, 0, 2).reshape(token_count, query_cols)
    live = (index < lengths[0])[:, None]
    return jnp.where(live, mixed, 0.0).astype(jnp.bfloat16)[None]


def solution(mesh):
    in_specs = (
        P("group", "tensor", None),
        P("group", None, "tensor"),
        P("group", None, None, None),
        P("group", None, None, None),
        P("tensor"),
        P(),
        P(),
        P(),
        P("group"),
    )
    out_specs = P("group", None, "tensor")
    return jax.shard_map(
        per_device, mesh=mesh, in_specs=in_specs, out_specs=out_specs, check_vma=False
    )
```

profile of v0, /device:TPU:57, one launch (start us, length us, event | category | flops | bytes accessed | tf_op | source)
XLA Modules:
  0.0 599.4 jit_solution(14467278969102455105)
XLA Ops:
  6.5 0.0 copy-start
  6.5 0.0 all-gather.7.cloned.1.call-start
  6.5 2.3 copy.34
  8.8 0.0 all-gather.7.cloned.1.call-update
  8.9 0.0 all-gather.11.cloned.1.call-start
  8.9 0.0 copy-done
  9.0 0.6 copy.46
  9.6 0.0 all-gather.11.cloned.1.call-update
  9.6 0.0 all-gather.9.cloned.1.call-start
  9.7 0.7 all-gather.9.cloned.1.call-update
  10.4 0.0 all-gather.13.cloned.1.call-start
  10.4 0.0 copy-done.8
  10.5 0.6 copy.47
  11.1 0.0 all-gather.13.cloned.1.call-update
  11.1 0.0 copy-done.10
  11.1 0.8 scatter_custom_fusion
  12.0 2.9 fusion.55
  14.9 0.1 broadcast_compare_fusion.2
  15.0 0.9 iota_compare_fusion
  16.6 0.7 fusion.110
  17.3 0.8 broadcast_compare_fusion.1
  18.1 0.8 broadcast_compare_fusion
  18.9 167.7 %all-gather.7.cloned.1.call-done = bf16[1,1024,4096]{1,2,0:T(8,128)(2,1)} async-done(((bf16[1,128,4096]{1,2,0:T(8,128)(2,1)}), bf16[1,1024,4096]{1,2,0:T(8,128)(2,1)}) %all-gather.7.cloned.1.call-update) | async-done | bytes 8388624 | tf_op jit(solution)/shard_map/all_gather | solution.py:39
  186.7 8.9 %gather_fusion = bf16[64,1024,64]{1,2,0:T(8,128)(2,1)} fusion(bf16[1024,64,64]{0,2,1:T(8,128)(2,1)} %bitcast.67, s32[1024]{0:T(1024)S(1)} %pad_clamp_fusion), kind=kCustom, calls=%fused_computation | custom fusion | bytes 16777472 | tf_op jit(solution)/shard_map/jit(_take)/gather | solution.py:56
  195.6 122.6 %all-gather.11.cloned.1.call-done = bf16[64,64,1,128]{3,1,2,0:T(8,128)(2,1)} async-done(((bf16[1,64,1,128]{3,1,2,0:T(8,128)(2,1)}), bf16[64,64,1,128]{3,1,2,0:T(8,128)(2,1)}) %all-gather.11.cloned.1.call-update) | async-done | bytes 1048592 | tf_op jit(solution)/shard_map/all_gather | solution.py:66
  318.2 5.0 fusion.36
  323.3 1.2 fusion.84
  324.5 0.7 copy.37
  325.2 112.7 %all-gather.9.cloned.1.call-done = bf16[64,64,512]{2,1,0:T(8,128)(2,1)} async-done(((bf16[1,64,512]{2,1,0:T(8,128)(2,1)}), bf16[64,64,512]{2,1,0:T(8,128)(2,1)}) %all-gather.9.cloned.1.call-update) | async-done | bytes 4194320 | tf_op jit(solution)/shard_map/all_gather | solution.py:60
  437.9 0.0 copy-done.9
  437.9 10.5 %bitcast_add_fusion = f32[1024,512]{0,1:T(8,128)} fusion(bf16[64,64,512]{2,1,0:T(8,128)(2,1)} %all-gather.9.cloned.1.call-done, f32[512]{0:T(512)S(1)} %copy-done.9, bf16[64,1024,64]{1,2,0:T(8,128)(2,1)} %gather_fusion, pred[64]{0:T(512)(128)(4,1)S(1)} %compare_and_fusion), kind=kOutput, calls=%fused_computation.24 | convolution fusion | flops 4299685888 | bytes 14682176 | tf_op jit(solution)/shard_map/tgc,gcn->tn/dot_general | solution.py:57
  448.3 2.1 copy.35
  450.4 0.6 fusion.81
  451.1 2.9 subtract_convert_fusion
  454.0 1.6 fusion.138
  455.6 0.0 copy-done.1
  455.6 1.2 fusion.26
  456.9 98.5 %all-gather.13.cloned.1.call-done = bf16[64,64,1,128]{3,1,2,0:T(8,128)(2,1)} async-done(((bf16[1,64,1,128]{3,1,2,0:T(8,128)(2,1)}), bf16[64,64,1,128]{3,1,2,0:T(8,128)(2,1)}) %all-gather.13.cloned.1.call-update) | async-done | bytes 1048592 | tf_op jit(solution)/shard_map/all_gather | solution.py:72
  555.3 6.4 %fusion.42 = bf16[1024,128]{1,0:T(8,128)(2,1)S(1)} fusion(bf16[64,64,1,128]{3,1,2,0:T(8,128)(2,1)} %all-gather.13.cloned.1.call-done, f32[128]{0:T(128)S(1)} %get-tuple-element.16, bf16[64,1024,64]{1,2,0:T(8,128)(2,1)} %gather_fusion, pred[64]{0:T(512)(128)(4,1)S(1)} %compare_and_fusion), kind=kOutput, calls=%fused_computation.48 | convolution fusion | flops 1078198272 | bytes 9699904 | tf_op jit(solution)/shard_map/tgc,gcn->tn/dot_general | solution.py:69
  561.8 0.0 copy-start.3
  561.8 0.7 fusion.80
  562.5 0.0 copy-done.3
  562.6 0.7 pad_maximum_fusion
  563.3 1.7 copy.40
  564.9 1.1 copy.41
  566.0 2.3 fusion.58
  568.3 1.1 copy.42
  569.5 2.7 fusion.52
  572.2 2.0 fusion.133
  574.2 0.0 slice-done.1
  574.2 0.0 copy-done.7
  574.2 3.6 fusion.50
  577.8 6.1 %fusion.132 = (f32[4,256]{1,0:T(4,128)S(1)}, f32[4,256,768]{2,1,0:T(8,128)}) fusion(f32[4,256,768]{2,1,0:T(8,128)} %fusion.58, pred[256,768]{1,0:T(8,128)(4,1)} %broadcast_compare_fusion), kind=kOutput, calls=%fused_computation.136 | output fusion | flops 4719359 | bytes 6492160 | tf_op jit(solution)/shard_map/sub | solution.py:122
  584.0 2.0 fusion.131
  586.0 0.0 slice-start
  586.0 1.1 fusion.16
  587.1 0.0 slice-start.2
  587.1 0.5 fusion.56
  587.6 0.4 slice-done.2
  588.1 2.6 fusion.23
  590.7 0.1 maximum_bitcast_fusion
  590.7 0.5 copy.43
  591.3 0.3 fusion.12
  591.6 1.3 copy.44
  (34 shorter events, 0.2 us)
Async XLA Ops:
  6.5 2.4 copy-start
  6.5 3.9 copy-start.8
  6.5 4.6 copy-start.10
  6.5 180.1 %all-gather.7.cloned.1.call-start = ((), (), s32[]{:S(2)}) async-start(), calls=%async_computation | async-start | bytes 9437184 | tf_op jit(solution)/shard_map/all_gather | solution.py:39
  8.9 309.4 %all-gather.11.cloned.1.call-start = ((), (), s32[]{:S(2)}) async-start(), calls=%async_computation.2 | async-start | bytes 1064960 | tf_op jit(solution)/shard_map/all_gather | solution.py:66
  9.6 428.3 %all-gather.9.cloned.1.call-start = ((), (), s32[]{:S(2)}) async-start(), calls=%async_computation.1 | async-start | bytes 4259840 | tf_op jit(solution)/shard_map/all_gather | solution.py:60
  10.4 545.0 %all-gather.13.cloned.1.call-start = ((), (), s32[]{:S(2)}) async-start(), calls=%async_computation.3 | async-start | bytes 1064960 | tf_op jit(solution)/shard_map/all_gather | solution.py:72
  318.2 119.7 %copy-start.9 = (f32[512]{0:T(512)S(1)}, f32[512]{0:T(512)}, u32[]{:S(2)}) copy-start(f32[512]{0:T(512)} %param.13) | copy-start | bytes 6148
  454.0 1.6 copy-start.1
  561.8 0.8 copy-start.3
  572.2 2.0 slice-start.1
  572.2 2.0 copy-start.7
  577.8 6.1 %copy-start.2 = (f32[4,256,1024]{2,1,0:T(8,128)S(1)}, f32[4,256,1024]{2,1,0:T(8,128)}, u32[]{:S(2)}) copy-start(f32[4,256,1024]{2,1,0:T(8,128)} %fusion.52) | copy-start | bytes 12582916
  577.8 6.1 %copy-start.5 = (pred[256,1024]{1,0:T(8,128)(4,1)S(1)}, pred[256,1024]{1,0:T(8,128)(4,1)}, u32[]{:S(2)}) copy-start(pred[256,1024]{1,0:T(8,128)(4,1)} %iota_compare_fusion) | copy-start | bytes 786436
  584.0 2.1 copy-start.4
  586.0 1.1 slice-start
  587.1 0.9 slice-start.2
  588.1 2.6 copy-start.6
Sparse Core Ops, SparseCore 0:
  10.4 176.2 all-gather.6
  188.8 129.3 all-gather.10
  320.4 117.4 all-gather.8
  439.9 115.4 all-gather.12
where the time goes:
time: 600 us; the launch traced here: 599 us
  waiting for transfers between devices  502 us (84%)
  matrix products  39.6 us (7%)
  local copies, waits for them, and re-layouts  23.1 us (4%)
  other arithmetic  20.3 us (3%)
  between operations  14.1 us (2%)
    all_gather x1, waiting for transfers between devices, per_device(): gathered = lax.all_gather(turns, 'tensor', axis=1, tiled=True)[0]  168 us
    all_gather x1, waiting for transfers between devices, per_device(): lax.all_gather(keys_mine, 'group', axis=0, tiled=True)  123 us
    all_gather x1, waiting for transfers between devices, per_device(): lax.all_gather(query_store, 'group', axis=0, tiled=True)  113 us
    all_gather x1, waiting for transfers between devices, per_device(): lax.all_gather(values_mine, 'group', axis=0, tiled=True)  98.5 us
  transfers between devices with their start and end apart: 4, of which 4 were waited for; matrix products, arithmetic and copies ran while one was open for 7% of the time, Pallas kernels for 0%

commit v1 on v0

--- a/solution.py
+++ b/solution.py
@@ -1,12 +1,23 @@
+import functools
 import jax
 import jax.numpy as jnp
 from jax import lax
 from jax.sharding import PartitionSpec as P
+from jax.lax import all_to_all, psum
 
 QUERY_HEADS = 32
 KEY_VALUE_HEADS = 4
 HEAD_SIZE = 128
 rotary_base = 1000000.0
+
+
+def _list_strings(here_x, join_dim):
+    return jnp.concatenate(
+        all_to_all(jnp.stack([here_x for _ in range(psum(1, "group"))], 0), "group", 0, 0), join_dim
+    )
+
+
+_raise_heads = functools.partial(_list_strings, join_dim=0)
 
 
 def rotary(heads, positions):
@@ -67,10 +78,7 @@
         preferred_element_type=jnp.float32,
     )
     proj_value = jnp.einsum(
-        "tgc,gcn->tn",
-        ordered,
-        lax.all_gather(values_mine, "group", axis=0, tiled=True),
-        preferred_element_type=jnp.float32,
+        "tgc,gcn->tn", ordered, _raise_heads(values_mine), preferred_element_type=jnp.float32
     )
     key_bias_rows = lax.dynamic_slice_in_dim(
         key_projection_bias.reshape(KEY_VALUE_HEADS, HEAD_SIZE),

time: 600 us -> 513 us (0.85)
  waiting for transfers between devices: 502 us -> 399 us
  starting transfers between devices: 0.12 us -> 14.9 us
    all_gather x1 -> x0, waiting for transfers between devices: 98.5 us -> none  [per_device(): lax.all_gather(values_mine, 'group', axis=0, tiled=True)]
    all_to_all x0 -> x1, starting transfers between devices: none -> 14.8 us  [_list_strings(): all_to_all(jnp.stack([here_x for _ in range(psum(1, 'group'))], 0), 'grou...]
  transfers between devices with their start and end apart: 4 -> 4, of which waited for: 4 -> 3; matrix products, arithmetic and copies ran while one was open for 7% -> 9% of each run, Pallas kernels for 0% -> 0%
where the time goes in v1:
time: 513 us; the launch traced here: 512 us
  waiting for transfers between devices  399 us (78%)
  matrix products  39.6 us (8%)
  local copies, waits for them, and re-layouts  24.4 us (5%)
  other arithmetic  20.4 us (4%)
  starting transfers between devices  14.9 us (3%)
  between operations  14.1 us (3%)
    all_gather x1, waiting for transfers between devices, per_device(): gathered = lax.all_gather(turns, 'tensor', axis=1, tiled=True)[0]  163 us
    all_gather x1, waiting for transfers between devices, per_device(): lax.all_gather(keys_mine, 'group', axis=0, tiled=True)  123 us
    all_gather x1, waiting for transfers between devices, per_device(): lax.all_gather(query_store, 'group', axis=0, tiled=True)  113 us
    all_to_all x1, starting transfers between devices, _list_strings(): all_to_all(jnp.stack([here_x for _ in range(psum(1, 'group'))], 0), 'grou...  14.8 us
    dot_general x1, matrix products, per_device(): jnp.einsum('tgc,gcn->tn', ordered, lax.all_gather(query_store, 'group', a...  10.5 us
  transfers between devices with their start and end apart: 4, of which 3 were waited for; matrix products, arithmetic and copies ran while one was open for 9% of the time, Pallas kernels for 0%

profile of v1, /device:TPU:57, one launch (start us, length us, event | category | flops | bytes accessed | tf_op | source)
XLA Modules:
  0.0 512.1 jit_solution(10293755158632685279)
XLA Ops:
  6.5 0.0 copy-start
  6.5 0.0 all-gather.5.cloned.1.call-start
  6.5 2.3 copy.33
  8.8 0.0 all-gather.5.cloned.1.call-update
  8.9 0.0 all-gather.9.cloned.1.call-start
  8.9 0.0 copy-done
  9.0 0.6 copy.45
  9.6 0.0 all-gather.9.cloned.1.call-update
  9.6 0.0 all-gather.7.cloned.1.call-start
  9.7 0.7 all-gather.7.cloned.1.call-update
  10.4 0.0 copy-done.8
  10.4 1.3 stack.3
  11.7 14.8 %all-to-all-start = ((bf16[64,1,64,128]{3,2,1,0:T(8,128)(2,1)}), bf16[64,1,64,128]{3,2,1,0:T(8,128)(2,1)}, u32[]{:S(2)}, u32[]{:S(2)}) async-start(bf16[64,1,64,128]{3,2,1,0:T(8,128)(2,1)} %stack.3), calls=%async_computation | async-start | bytes 2097152 | tf_op jit(solution)/shard_map/all_to_all | solution.py:16
  27.3 0.0 copy-done.10
  27.3 0.8 scatter_custom_fusion
  28.1 0.7 fusion.110
  28.8 0.7 fusion.111
  29.5 0.1 broadcast_compare_fusion.2
  29.6 0.8 broadcast_compare_fusion.1
  30.4 0.9 broadcast_compare_fusion
  31.3 0.9 iota_compare_fusion
  32.2 2.8 fusion.55
  35.1 162.6 %all-gather.5.cloned.1.call-done = bf16[1,1024,4096]{1,2,0:T(8,128)(2,1)} async-done(((bf16[1,128,4096]{1,2,0:T(8,128)(2,1)}), bf16[1,1024,4096]{1,2,0:T(8,128)(2,1)}) %all-gather.5.cloned.1.call-update) | async-done | bytes 8388624 | tf_op jit(solution)/shard_map/all_gather | solution.py:50
  197.7 8.9 %gather_fusion = bf16[64,1024,64]{1,2,0:T(8,128)(2,1)} fusion(bf16[1024,64,64]{0,2,1:T(8,128)(2,1)} %bitcast.70, s32[1024]{0:T(1024)S(1)} %pad_clamp_fusion), kind=kCustom, calls=%fused_computation | custom fusion | bytes 16777472 | tf_op jit(solution)/shard_map/jit(_take)/gather | solution.py:67
  206.6 122.7 %all-gather.9.cloned.1.call-done = bf16[64,64,1,128]{3,1,2,0:T(8,128)(2,1)} async-done(((bf16[1,64,1,128]{3,1,2,0:T(8,128)(2,1)}), bf16[64,64,1,128]{3,1,2,0:T(8,128)(2,1)}) %all-gather.9.cloned.1.call-update) | async-done | bytes 1048592 | tf_op jit(solution)/shard_map/all_gather | solution.py:77
  329.3 5.0 fusion.36
  334.3 1.2 fusion.84
  335.5 0.7 copy.36
  336.2 112.7 %all-gather.7.cloned.1.call-done = bf16[64,64,512]{2,1,0:T(8,128)(2,1)} async-done(((bf16[1,64,512]{2,1,0:T(8,128)(2,1)}), bf16[64,64,512]{2,1,0:T(8,128)(2,1)}) %all-gather.7.cloned.1.call-update) | async-done | bytes 4194320 | tf_op jit(solution)/shard_map/all_gather | solution.py:71
  448.9 0.0 copy-done.9
  448.9 10.5 %bitcast_add_fusion = f32[1024,512]{0,1:T(8,128)} fusion(bf16[64,64,512]{2,1,0:T(8,128)(2,1)} %all-gather.7.cloned.1.call-done, f32[512]{0:T(512)S(1)} %copy-done.9, bf16[64,1024,64]{1,2,0:T(8,128)(2,1)} %gather_fusion, pred[64]{0:T(512)(128)(4,1)S(1)} %compare_and_fusion), kind=kOutput, calls=%fused_computation.24 | convolution fusion | flops 4299685888 | bytes 14682176 | tf_op jit(solution)/shard_map/tgc,gcn->tn/dot_general | solution.py:68
  459.4 2.1 copy.34
  461.5 0.7 fusion.81
  462.1 2.9 subtract_convert_fusion
  465.1 1.6 fusion.138
  466.7 0.0 copy-done.1
  466.7 1.2 fusion.26
  467.9 0.0 all-to-all-done
  467.9 6.4 %fusion.42 = bf16[1024,128]{1,0:T(8,128)(2,1)S(1)} fusion(bf16[64,1,64,128]{3,2,1,0:T(8,128)(2,1)} %all-to-all-done, f32[128]{0:T(128)S(1)} %fusion.111, bf16[64,1024,64]{1,2,0:T(8,128)(2,1)} %gather_fusion, pred[64]{0:T(512)(128)(4,1)S(1)} %compare_and_fusion), kind=kOutput, calls=%fused_computation.48 | convolution fusion | flops 1078198272 | bytes 9699904 | tf_op jit(solution)/shard_map/tgc,gcn->tn/dot_general | solution.py:80
  474.4 0.0 copy-start.3
  474.4 0.8 fusion.80
  475.1 0.0 copy-done.3
  475.2 0.7 pad_maximum_fusion
  475.9 1.7 copy.39
  477.6 1.1 copy.40
  478.6 2.3 fusion.58
  480.9 1.1 copy.41
  482.1 2.7 fusion.52
  484.8 2.0 fusion.133
  486.8 0.0 slice-done.1
  486.8 3.6 fusion.50
  490.5 6.1 %fusion.132 = (f32[4,256]{1,0:T(4,128)S(1)}, f32[4,256,768]{2,1,0:T(8,128)}) fusion(f32[4,256,768]{2,1,0:T(8,128)} %fusion.58, pred[256,768]{1,0:T(8,128)(4,1)} %broadcast_compare_fusion), kind=kOutput, calls=%fused_computation.137 | output fusion | flops 4719359 | bytes 6492160 | tf_op jit(solution)/shard_map/sub | solution.py:130
  496.6 2.0 fusion.131
  498.7 0.0 slice-start
  498.7 1.1 fusion.16
  499.7 0.0 slice-done
  499.8 0.0 slice-start.2
  499.8 0.5 fusion.56
  500.3 0.4 slice-done.2
  500.7 2.6 fusion.23
  503.3 0.1 maximum_bitcast_fusion
  503.4 0.5 copy.42
  503.9 0.3 fusion.12
  504.2 1.3 copy.43
  (35 shorter events, 0.2 us)
Async XLA Ops:
  6.5 2.4 copy-start
  6.5 3.8 copy-start.8
  6.5 20.7 %copy-start.10 = (s32[64]{0:T(128)S(1)}, s32[64]{0:T(128)}, u32[]{:S(2)}) copy-start(s32[64]{0:T(128)} %param.16) | copy-start | bytes 772
  6.5 191.1 %all-gather.5.cloned.1.call-start = ((), (), s32[]{:S(2)}) async-start(), calls=%async_computation.1 | async-start | bytes 9437184 | tf_op jit(solution)/shard_map/all_gather | solution.py:50
  8.9 320.4 %all-gather.9.cloned.1.call-start = ((), (), s32[]{:S(2)}) async-start(), calls=%async_computation.3 | async-start | bytes 1064960 | tf_op jit(solution)/shard_map/all_gather | solution.py:77
  9.6 439.3 %all-gather.7.cloned.1.call-start = ((), (), s32[]{:S(2)}) async-start(), calls=%async_computation.2 | async-start | bytes 4259840 | tf_op jit(solution)/shard_map/all_gather | solution.py:71
  11.7 456.2 %all-to-all-start = ((bf16[64,1,64,128]{3,2,1,0:T(8,128)(2,1)}), bf16[64,1,64,128]{3,2,1,0:T(8,128)(2,1)}, u32[]{:S(2)}, u32[]{:S(2)}) async-start(bf16[64,1,64,128]{3,2,1,0:T(8,128)(2,1)} %stack.3), calls=%async_computation | async-start | bytes 2097152 | tf_op jit(solution)/shard_map/all_to_all | solution.py:16
  206.6 242.3 %copy-start.9 = (f32[512]{0:T(512)S(1)}, f32[512]{0:T(512)}, u32[]{:S(2)}) copy-start(f32[512]{0:T(512)} %param.13) | copy-start | bytes 6148
  465.1 1.6 copy-start.1
  474.4 0.8 copy-start.3
  484.8 2.0 slice-start.1
  484.8 2.0 copy-start.7
  490.5 6.1 %copy-start.2 = (f32[4,256,1024]{2,1,0:T(8,128)S(1)}, f32[4,256,1024]{2,1,0:T(8,128)}, u32[]{:S(2)}) copy-start(f32[4,256,1024]{2,1,0:T(8,128)} %fusion.52) | copy-start | bytes 12582916
  490.5 6.1 %copy-start.5 = (pred[256,1024]{1,0:T(8,128)(4,1)S(1)}, pred[256,1024]{1,0:T(8,128)(4,1)}, u32[]{:S(2)}) copy-start(pred[256,1024]{1,0:T(8,128)(4,1)} %iota_compare_fusion) | copy-start | bytes 786436
  496.6 2.1 copy-start.4
  498.7 1.1 slice-start
  499.8 0.9 slice-start.2
  500.7 2.6 copy-start.6
Sparse Core Ops, SparseCore 0:
  10.4 187.2 all-gather.4
  199.8 129.3 all-gather.8
  331.4 117.4 all-gather.6
